TPU v7x, 32 devices: a whole 2x2x4 slice. The times are simulated.
32 devices in a mesh: dp: 8 (over z, x), mp: 4 (over y, core).
Axes of the slice: x: 2, y: 2, z: 4, core: 2. Of those that a mesh axis runs over, the one named last changes fastest.
Arguments:
- inputs: bfloat16 [16384, 768], P('dp'), may hold values from -6 to 6
- segments: int32 [256, 64], P('dp'), may hold values from 0 to 5, never falling along the last dimension, each value on 1 to 24 neighbouring positions
- cotangent: bfloat16 [16384, 768], P('dp'), may hold values from -12 to 12
- triple_weight: float32 [3, 768, 768], P(None, 'dp', 'mp'), may hold values from -0.21875 to 0.21875
- triple_first: float32 [3, 768, 768], P(None, 'dp', 'mp')
- triple_second: float32 [3, 768, 768], P(None, 'dp', 'mp'), as said below
- outward_weight: float32 [768, 768], P('mp', 'dp'), may hold values from -0.625 to 0.625
- outward_first: float32 [768, 768], P('mp', 'dp')
- outward_second: float32 [768, 768], P('mp', 'dp'), as said below
- expand_weight: float32 [768, 3072], P('dp', 'mp'), may hold values from -2 to 2
- expand_first: float32 [768, 3072], P('dp', 'mp')
- expand_second: float32 [768, 3072], P('dp', 'mp'), as said below
- reduce_weight: float32 [3072, 768], P('mp', 'dp'), may hold values from -0.109375 to 0.109375
- reduce_first: float32 [3072, 768], P('mp', 'dp')
- reduce_second: float32 [3072, 768], P('mp', 'dp'), as said below
- norm_params: float32 [6, 768], replicated, may hold values from -3 to 4
- norm_first: float32 [6, 768], replicated
- norm_second: float32 [6, 768], replicated, as said below
- paired_bias: float32 [2, 768], P(None, 'mp'), may hold values from -1.8 to 1.8
- paired_first: float32 [2, 768], P(None, 'mp')
- paired_second: float32 [2, 768], P(None, 'mp'), as said below
- hidden_bias: float32 [3072], P('mp'), may hold values from -1.8 to 1.8
- hidden_first: float32 [3072], P('mp')
- hidden_second: float32 [3072], P('mp'), as said below
Outputs:
- outputs: bfloat16 [16384, 768], P('dp')
- input_gradient: bfloat16 [16384, 768], P('dp')
- gradient_norm: float32 [], replicated
- triple_moment: float32 [3, 768, 768], P(None, 'dp', 'mp')
- triple_square: float32 [3, 768, 768], P(None, 'dp', 'mp')
- triple_updated: float32 [3, 768, 768], P(None, 'dp', 'mp')
- outward_moment: float32 [768, 768], P('mp', 'dp')
- outward_square: float32 [768, 768], P('mp', 'dp')
- outward_updated: float32 [768, 768], P('mp', 'dp')
- expand_moment: float32 [768, 3072], P('dp', 'mp')
- expand_square: float32 [768, 3072], P('dp', 'mp')
- expand_updated: float32 [768, 3072], P('dp', 'mp')
- reduce_moment: float32 [3072, 768], P('mp', 'dp')
- reduce_square: float32 [3072, 768], P('mp', 'dp')
- reduce_updated: float32 [3072, 768], P('mp', 'dp')
- norm_moment: float32 [6, 768], replicated
- norm_square: float32 [6, 768], replicated
- norm_updated: float32 [6, 768], replicated
- paired_moment: float32 [2, 768], P(None, 'mp')
- paired_square: float32 [2, 768], P(None, 'mp')
- paired_updated: float32 [2, 768], P(None, 'mp')
- hidden_moment: float32 [3072], P('mp')
- hidden_square: float32 [3072], P('mp')
- hidden_updated: float32 [3072], P('mp')
Inputs may be any that keep to these rules, and one draw needn't show every extreme that they name: `segments`: within each row of 64 tokens the numbers never fall; each of the 6 captions holds 1 to 24 tokens, one exactly 24. `triple_second`: positive. `outward_second`: positive. `expand_second`: positive. `reduce_second`: positive. `norm_second`: positive. `paired_second`: positive. `hidden_second`: positive.
All inputs are finite; a program needn't handle non-finite values.
Results may differ from a plain program's by a relative error of at most 0.02.
Values may be sent and summed in bfloat16 or wider, within the bound.
No kernel may reach another device: no remote copies, remote signals or barrier semaphores. Data moves between devices by JAX's collectives and lax.ppermute only.
A program may use at most 128 MiB of HBM per device.

v0:
```python
import jax
import jax.numpy as jnp
from jax import lax
from jax.sharding import PartitionSpec as P

HD = 64
STEP = 5
EPS_NORM = 1e-06
BETA = 0.5
LR_MATRIX = 0.03
LR_VECTOR = 0.2
DECAY = 0.1
ADAM_EPS = 1e-08
CLIP = 1.0
NEG = -1e30


def norm_forward(rows_in, gain_row, shift_row):
    row_mean = jnp.mean(rows_in, axis=-1, keepdims=True)
    centred = rows_in - row_mean
    variance = jnp.mean(centred * centred, axis=-1, keepdims=True)
    scaled = lax.rsqrt(variance + EPS_NORM)
    normal_rows = centred * scaled
    return (normal_rows * gain_row + shift_row, normal_rows, scaled)


def norm_backward(upstream, normal_rows, scaled, gain_row):
    gained = upstream * gain_row
    mean_one = jnp.mean(gained, axis=-1, keepdims=True)
    mean_two = jnp.mean(gained * normal_rows, axis=-1, keepdims=True)
    return scaled * (gained - mean_one - normal_rows * mean_two)


def smooth_gate(values_in):
    return jax.nn.gelu(values_in, approximate=True)


def adam_step(weight, first, second, grad, factor, rate, decay):
    clipped = grad * factor
    first_new = BETA * first + (1.0 - BETA) * clipped
    second_new = BETA * second + (1.0 - BETA) * clipped * clipped
    correction = 1.0 - BETA**STEP
    direction = first_new / correction / (jnp.sqrt(second_new / correction) + ADAM_EPS)
    return (first_new, second_new, weight - rate * (direction + decay * weight))


def per_device(
    inputs,
    segments,
    cotangent,
    triple_weight,
    triple_first,
    triple_second,
    outward_weight,
    outward_first,
    outward_second,
    expand_weight,
    expand_first,
    expand_second,
    reduce_weight,
    reduce_first,
    reduce_second,
    norm_params,
    norm_first,
    norm_second,
    paired_bias,
    paired_first,
    paired_second,
    hidden_bias,
    hidden_first,
    hidden_second,
):
    f32 = jnp.float32
    bf16 = jnp.bfloat16
    dp_count = lax.axis_size("dp")
    mp_count = lax.axis_size("mp")
    triple_full, outward_full, expand_full, reduce_full = (
        lax.all_gather(triple_weight.astype(bf16), "dp", axis=1, tiled=True),
        lax.all_gather(outward_weight.astype(bf16), "dp", axis=1, tiled=True),
        lax.all_gather(expand_weight.astype(bf16), "dp", axis=0, tiled=True),
        lax.all_gather(reduce_weight.astype(bf16), "dp", axis=1, tiled=True),
    )
    row_count, row_length = segments.shape
    token_count = inputs.shape[0]
    head_width = triple_full.shape[2]
    head_count = head_width // HD
    scale_factor = HD ** (-0.5)
    grid = (row_count, row_length, head_count, HD)
    x_full = inputs.astype(f32)
    normed_one, normal_one, scaled_one = norm_forward(x_full, norm_params[0], norm_params[1])
    first_low = normed_one.astype(bf16)
    projected = jnp.einsum("td,cdw->ctw", first_low, triple_full, preferred_element_type=f32)
    queries = (projected[0] + paired_bias[0]).astype(bf16).reshape(grid)
    key_rows = projected[1].astype(bf16).reshape(grid)
    value_rows = (projected[2] + paired_bias[1]).astype(bf16).reshape(grid)
    same_caption = (segments[:, :, None] == segments[:, None, :])[:, None, :, :]

    def scores_of(query_in, key_in):
        raw_scores = jnp.einsum("rqhd,rkhd->rhqk", query_in, key_in, preferred_element_type=f32)
        return jnp.where(same_caption, raw_scores * scale_factor, NEG)

    scores = scores_of(queries, key_rows)
    row_top = jnp.max(scores, axis=-1, keepdims=True)
    lifted = jnp.exp(scores - row_top)
    row_total = jnp.sum(lifted, axis=-1, keepdims=True)
    probs = lifted / row_total
    log_total = row_top + jnp.log(row_total)
    context = jnp.einsum(
        "rhqk,rkhd->rqhd", probs.astype(bf16), value_rows, preferred_element_type=f32
    )
    context_low = context.astype(bf16).reshape(token_count, head_width)
    attn_part = jnp.dot(context_low, outward_full, preferred_element_type=f32)
    attended = lax.psum(attn_part.astype(jnp.bfloat16), "mp").astype(jnp.float32)
    middle = x_full + attended + norm_params[4]
    normed_two, normal_two, scaled_two = norm_forward(middle, norm_params[2], norm_params[3])
    second_low = normed_two.astype(bf16)
    hidden_pre = jnp.dot(second_low, expand_full, preferred_element_type=f32) + hidden_bias
    gate_out, gelu_pull = jax.vjp(smooth_gate, hidden_pre)
    activated = gate_out.astype(bf16)
    fed_part = jnp.dot(activated, reduce_full, preferred_element_type=f32)
    fed = lax.psum(fed_part.astype(jnp.bfloat16), "mp").astype(jnp.float32)
    outputs = (middle + fed + norm_params[5]).astype(bf16)
    cot_full = cotangent.astype(f32)
    grad_reduce = jnp.einsum("tf,td->fd", activated, cotangent, preferred_element_type=f32)
    act_grad = jnp.einsum("td,fd->tf", cotangent, reduce_full, preferred_element_type=f32)
    hidden_grad = gelu_pull(act_grad)[0].astype(bf16)
    grad_expand = jnp.einsum("td,tf->df", second_low, hidden_grad, preferred_element_type=f32)
    grad_hidden = jnp.sum(hidden_grad, axis=0, dtype=f32)
    second_part = jnp.einsum("tf,df->td", hidden_grad, expand_full, preferred_element_type=f32)
    second_grad = lax.psum(second_part.astype(jnp.bfloat16), "mp").astype(jnp.float32)
    middle_grad = cot_full + norm_backward(second_grad, normal_two, scaled_two, norm_params[2])
    middle_low = middle_grad.astype(bf16)
    grad_outward = jnp.einsum("tw,td->wd", context_low, middle_low, preferred_element_type=f32)
    context_grad = (
        jnp.einsum("td,wd->tw", middle_low, outward_full, preferred_element_type=f32)
        .astype(bf16)
        .reshape(grid)
    )
    probs_again = jnp.exp(scores_of(queries, key_rows) - log_total)
    probs_low = probs_again.astype(bf16)
    value_grad = jnp.einsum(
        "rhqk,rqhd->rkhd", probs_low, context_grad, preferred_element_type=f32
    ).astype(bf16)
    prob_grad = jnp.einsum("rqhd,rkhd->rhqk", context_grad, value_rows, preferred_element_type=f32)
    inner = jnp.sum(prob_grad * probs_again, axis=-1, keepdims=True)
    score_grad = (probs_again * (prob_grad - inner) * scale_factor).astype(bf16)
    query_grad = jnp.einsum(
        "rhqk,rkhd->rqhd", score_grad, key_rows, preferred_element_type=f32
    ).astype(bf16)
    key_grad = jnp.einsum(
        "rhqk,rqhd->rkhd", score_grad, queries, preferred_element_type=f32
    ).astype(bf16)
    stacked = jnp.stack([query_grad, key_grad, value_grad]).reshape(3, token_count, head_width)
    grad_triple = jnp.einsum("td,ctw->cdw", first_low, stacked, preferred_element_type=f32)
    grad_paired = jnp.stack(
        [jnp.sum(stacked[0], axis=0, dtype=f32), jnp.sum(stacked[2], axis=0, dtype=f32)]
    )
    first_part = jnp.einsum("ctw,cdw->td", stacked, triple_full, preferred_element_type=f32)
    first_grad = lax.psum(first_part.astype(jnp.bfloat16), "mp").astype(jnp.float32)
    input_gradient = (
        middle_grad + norm_backward(first_grad, normal_one, scaled_one, norm_params[0])
    ).astype(bf16)
    grad_norms = jnp.stack(
        [
            jnp.sum(first_grad * normal_one, axis=0),
            jnp.sum(first_grad, axis=0),
            jnp.sum(second_grad * normal_two, axis=0),
            jnp.sum(second_grad, axis=0),
            jnp.sum(middle_grad, axis=0),
            jnp.sum(cot_full, axis=0),
        ]
    )
    owned = (
        lax.psum_scatter(grad_triple, "dp", scatter_dimension=1, tiled=True),
        lax.psum_scatter(grad_outward, "dp", scatter_dimension=1, tiled=True),
        lax.psum_scatter(grad_expand, "dp", scatter_dimension=0, tiled=True),
        lax.psum_scatter(grad_reduce, "dp", scatter_dimension=1, tiled=True),
    )
    vectors = lax.psum((grad_norms, grad_paired, grad_hidden), "dp")
    local_square = jnp.zeros((), f32)
    for grad_item in owned:
        local_square = local_square + jnp.sum(grad_item * grad_item)
    local_square = local_square + jnp.sum(vectors[0] * vectors[0]) / (dp_count * mp_count)
    local_square = (
        local_square
        + (jnp.sum(vectors[1] * vectors[1]) + jnp.sum(vectors[2] * vectors[2])) / dp_count
    )
    total_square = lax.psum(local_square, ("dp", "mp"))
    gradient_norm = jnp.sqrt(total_square)
    factor = jnp.minimum(1.0, CLIP / gradient_norm)
    triple_new = adam_step(
        triple_weight, triple_first, triple_second, owned[0], factor, LR_MATRIX, DECAY
    )
    outward_new = adam_step(
        outward_weight, outward_first, outward_second, owned[1], factor, LR_MATRIX, DECAY
    )
    expand_new = adam_step(
        expand_weight, expand_first, expand_second, owned[2], factor, LR_MATRIX, DECAY
    )
    reduce_new = adam_step(
        reduce_weight, reduce_first, reduce_second, owned[3], factor, LR_MATRIX, DECAY
    )
    norm_new = adam_step(norm_params, norm_first, norm_second, vectors[0], factor, LR_VECTOR, 0.0)
    paired_new = adam_step(
        paired_bias, paired_first, paired_second, vectors[1], factor, LR_VECTOR, 0.0
    )
    hidden_new = adam_step(
        hidden_bias, hidden_first, hidden_second, vectors[2], factor, LR_VECTOR, 0.0
    )
    return (
        outputs,
        input_gradient,
        gradient_norm,
        triple_new[0],
        triple_new[1],
        triple_new[2],
        outward_new[0],
        outward_new[1],
        outward_new[2],
        expand_new[0],
        expand_new[1],
        expand_new[2],
        reduce_new[0],
        reduce_new[1],
        reduce_new[2],
        norm_new[0],
        norm_new[1],
        norm_new[2],
        paired_new[0],
        paired_new[1],
        paired_new[2],
        hidden_new[0],
        hidden_new[1],
        hidden_new[2],
    )


def solution(mesh):
    placed = (
        P("dp", None),
        P("dp", None),
        P("dp", None),
        P(None, "dp", "mp"),
        P(None, "dp", "mp"),
        P(None, "dp", "mp"),
        P("mp", "dp"),
        P("mp", "dp"),
        P("mp", "dp"),
        P("dp", "mp"),
        P("dp", "mp"),
        P("dp", "mp"),
        P("mp", "dp"),
        P("mp", "dp"),
        P("mp", "dp"),
        P(),
        P(),
        P(),
        P(None, "mp"),
        P(None, "mp"),
        P(None, "mp"),
        P("mp"),
        P("mp"),
        P("mp"),
    )
    return jax.shard_map(
        per_device,
        mesh=mesh,
        in_specs=placed,
        out_specs=(
            P("dp", None),
            P("dp", None),
            P(),
            P(None, "dp", "mp"),
            P(None, "dp", "mp"),
            P(None, "dp", "mp"),
            P("mp", "dp"),
            P("mp", "dp"),
            P("mp", "dp"),
            P("dp", "mp"),
            P("dp", "mp"),
            P("dp", "mp"),
            P("mp", "dp"),
            P("mp", "dp"),
            P("mp", "dp"),
            P(),
            P(),
            P(),
            P(None, "mp"),
            P(None, "mp"),
            P(None, "mp"),
            P("mp"),
            P("mp"),
            P("mp"),
        ),
        check_vma=False,
    )
```

profile of v0, /device:TPU:0, one launch (start us, length us, event | category | flops | bytes accessed | tf_op | source)
XLA Modules:
  0.0 715.4 jit_solution(5087993690982692376)
XLA Ops:
  12.8 40.5 %all_gather.12 = bf16[3,768,192]{2,0,1:T(4,128)(2,1)} all-gather(bf16[3,96,192]{2,0,1:T(4,128)(2,1)S(1)} %copy.118), channel_id=1, replica_groups=mesh['dp'=8,'mp'=4] {'dp'}, dimensions={1}, use_global_device_ids=true | all-gather | bytes 995328 | tf_op jit(solution)/shard_map/all_gather | solution.py:78
  53.2 3.4 copy.119
  56.7 3.4 fusion.96
  65.1 31.9 %all_gather.13 = bf16[192,768]{0,1:T(8,128)(2,1)S(1)} all-gather(bf16[192,96]{0,1:T(8,128)(2,1)} %copy.127), channel_id=1, replica_groups=mesh['dp'=8,'mp'=4] {'dp'}, dimensions={1}, use_global_device_ids=true | all-gather | bytes 331776 | tf_op jit(solution)/shard_map/all_gather | solution.py:79
  97.0 3.4 convert_element_type.130
  100.4 3.4 copy.123
  103.8 3.6 squeeze.4
  107.4 3.9 copy.120
  111.3 3.6 squeeze.10
  114.9 5.7 fusion.108
  126.9 3.5 reshape.145
  130.4 3.9 convolution_convert_fusion.2
  138.0 63.8 %all-reduce.6.cloned.1.call-done = bf16[2048,768]{1,0:T(8,128)(2,1)} async-done(((bf16[2048,768]{1,0:T(8,128)(2,1)}), bf16[2048,768]{1,0:T(8,128)(2,1)}) %all-reduce.6.cloned.1.call-update) | async-done | bytes 3145744 | tf_op jit(solution)/shard_map/psum | solution.py:113
  201.8 3.1 fusion.46
  207.4 3.0 add_convert_fusion.1
  210.4 7.5 %fusion.111 = f32[2048,768]{1,0:T(8,128)} fusion(bf16[2048,768]{1,0:T(8,128)(2,1)} %add_convert_fusion.1, bf16[768,768]{1,0:T(8,128)(2,1)} %all-gather.3.cloned.1.call-done), kind=kOutput, calls=%fused_computation.161 | convolution fusion | flops 2415919104 | bytes 10616832 | tf_op jit(solution)/shard_map/dot_general | solution.py:117
  220.3 10.8 %convert_reduce_fusion.4 = (f32[768]{0:T(1024)}, bf16[2048,768]{1,0:T(8,128)(2,1)S(1)}, bf16[2048,768]{1,0:T(8,128)(2,1)}) fusion(f32[2048,768]{1,0:T(8,128)} %fusion.111, f32[768]{0:T(1024)} %param.45, bf16[2048,768]{1,0:T(8,128)(2,1)} %param.26, bf16[768,768]{0,1:T(8,128)(2,1)} %all-gather.5.cloned.1.call-done), kind=kOutput, calls=%fused_computation.46 | convolution fusion | flops 2455239936 | bytes 16914432 | tf_op jit(solution)/shard_map/td,fd->tf/dot_general | solution.py:125
  232.8 4.0 convolution_convert_fusion
  238.7 6.6 convolution_convert_fusion.1
  245.2 58.7 %all-reduce.8.cloned.1.call-done = bf16[2048,768]{1,0:T(8,128)(2,1)} async-done(((bf16[2048,768]{1,0:T(8,128)(2,1)}), bf16[2048,768]{1,0:T(8,128)(2,1)}) %all-reduce.8.cloned.1.call-update) | async-done | bytes 3145744 | tf_op jit(solution)/shard_map/psum | solution.py:130
  303.9 7.1 fusion.30
  311.1 4.7 fusion.106
  320.7 4.9 convolution_convert_fusion.3
  325.6 3.4 reshape.146
  329.0 3.6 copy.128
  332.7 5.1 fusion.81
  337.8 10.3 %fusion.71 = bf16[32,64,3,64]{1,3,2,0:T(8,128)(2,1)} fusion(f32[32,3,64,64]{2,3,1,0:T(8,128)} %fusion.81, f32[32,3,64,64]{2,3,1,0:T(8,128)} %copy-done.4, f32[32,3,64]{2,1,0:T(4,128)S(1)} %copy-done.23, f32[32,64,3,64]{1,0,3,2:T(8,128)} %squeeze.10, f32[3,64]{1,0:T(4,128)S(1)} %copy-done.47), kind=kOutput, calls=%fused_computation.91 | convolution fusion | flops 54270016 | bytes 5530368 | tf_op jit(solution)/shard_map/rhqk,rqhd->rkhd/dot_general | solution.py:150
  348.1 8.1 %convert_reduce_fusion.6 = (f32[3,64]{1,0:T(4,128)S(1)}, bf16[32,64,3,64]{3,1,2,0:T(8,128)(2,1)}) fusion(bf16[32,64,3,64]{3,1,2,0:T(8,128)(2,1)} %copy.123, f32[32,3,64,64]{2,3,1,0:T(8,128)} %fusion.81, f32[32,3,64,64]{2,3,1,0:T(8,128)} %copy-done.4, f32[32,3,64]{2,1,0:T(4,128)S(1)} %copy-done.23), kind=kOutput, calls=%fused_computation.60 | convolution fusion | flops 54269824 | bytes 4743936 | tf_op jit(solution)/shard_map/rhqk,rkhd->rqhd/dot_general | solution.py:147
  356.2 4.4 convert_reduce_fusion.5
  360.6 3.6 copy.131
  364.2 3.5 stack.42
  369.9 3.6 copy.133
  373.4 3.5 stack.43
  377.0 3.2 copy.135
  380.1 3.5 stack.44
  387.9 6.0 bitcast_convert_fusion
  394.0 7.1 fusion.112
  401.4 6.9 fusion.113
  408.4 5.2 fusion.65
  413.6 4.2 copy.149
  417.8 4.7 reshape.151
  429.0 85.0 %all-reduce.10.cloned.1.call-done = (bf16[2048,768]{1,0:T(8,128)(2,1)}, bf16[2048,768]{1,0:T(8,128)(2,1)}) async-done(((bf16[2048,768]{1,0:T(8,128)(2,1)}, bf16[2048,768]{1,0:T(8,128)(2,1)}), (bf16[2048,768]{1,0:T(8,128)(2,1)}, bf16[2048,768]{1,0:T(8,128)(2,1)})) %all-reduce.10.cloned.1.call-update) | async-done | bytes 6291472 | tf_op jit(solution)/shard_map/psum | solution.py:121
  514.0 4.6 fusion.31
  518.7 37.3 %all-reduce = (f32[6,768]{1,0:T(8,128)S(1)}, f32[2,192]{1,0:T(2,128)S(1)}, f32[768]{0:T(1024)S(1)}) all-reduce(f32[6,768]{1,0:T(8,128)S(1)} %stack.52, f32[2,192]{1,0:T(2,128)S(1)} %pad_maximum_fusion, f32[768]{0:T(1024)S(1)} %copy-done.53), channel_id=1, replica_groups=mesh['dp'=8,'mp'=4] {'dp'}, use_global_device_ids=true, to_apply=%region_29.30 | all-reduce | flops 5760 | bytes 46080 | tf_op jit(solution)/shard_map/psum | solution.py:179
  561.4 6.3 reduce-scatter.11.cloned.1.call-done
  570.5 67.2 %reduce-scatter.13.cloned.1.call-done = f32[96,576]{1,0:T(8,128)} async-done(((f32[768,576]{1,0:T(8,128)}), f32[96,576]{1,0:T(8,128)}) %reduce-scatter.13.cloned.1.call-update) | async-done | bytes 221200
  644.0 10.6 %fusion.16 = (bf16[2048,768]{1,0:T(8,128)(2,1)}, bf16[2048,768]{1,0:T(8,128)(2,1)}) fusion(f32[2048,768]{1,0:T(8,128)} %copy-done.3, bf16[2048,768]{1,0:T(8,128)(2,1)S(1)} %copy-done, bf16[2048,768]{1,0:T(8,128)(2,1)} %get-tuple-element.140, f32[2048]{0:T(1024)} %broadcast_multiply_fusion, f32[2048]{0:T(1024)} %broadcast_multiply_fusion.1, ...), kind=kLoop, calls=%fused_computation.29 | loop fusion | flops 28311552 | bytes 25207808 | tf_op jit(solution)/shard_map/convert_element_type | solution.py:162
  654.7 39.5 %psum.63 = f32[]{:T(128)} all-reduce(f32[]{:T(128)S(6)} %add.294), channel_id=1, replica_groups=mesh['dp'=8,'mp'=4] {'dp','mp'}, use_global_device_ids=true, to_apply=%region_38.39 | all-reduce | flops 1 | bytes 8 | tf_op jit(solution)/shard_map/psum | solution.py:188
  (201 shorter events, 68.1 us)
Async XLA Ops:
  8.1 193.7 %all-reduce.6.cloned.1.call-start = ((), (), s32[]{:S(2)}) async-start(), calls=%async_computation.4 | async-start | bytes 6291456 | tf_op jit(solution)/shard_map/psum | solution.py:113
  10.9 45.8 %copy-start.25 = (f32[2048]{0:T(1024)}, f32[2048]{0:T(1024)S(1)}, u32[]{:S(2)}) copy-start(f32[2048]{0:T(1024)S(1)} %broadcast_multiply_fusion.5) | copy-start | bytes 24580
  12.0 48.1 %copy-start.32 = (f32[2048]{0:T(1024)}, f32[2048]{0:T(1024)S(1)}, u32[]{:S(2)}) copy-start(f32[2048]{0:T(1024)S(1)} %add_rsqrt_fusion.1) | copy-start | bytes 24580
  12.6 47.5 %copy-start.35 = (f32[768]{0:T(1024)}, f32[768]{0:T(1024)S(1)}, u32[]{:S(2)}) copy-start(f32[768]{0:T(1024)S(1)} %get-tuple-element.133) | copy-start | bytes 9220
  12.6 47.5 %copy-start.54 = (f32[768]{0:T(1024)}, f32[768]{0:T(1024)S(1)}, u32[]{:S(2)}) copy-start(f32[768]{0:T(1024)S(1)} %get-tuple-element.132) | copy-start | bytes 9220
  63.2 58.3 %copy-start.44 = (f32[3,64]{1,0:T(4,128)}, f32[3,64]{1,0:T(4,128)S(1)}, u32[]{:S(2)}) copy-start(f32[3,64]{1,0:T(4,128)S(1)} %add.264) | copy-start | bytes 2308
  63.3 51.6 %copy-start.46 = (f32[3,64]{1,0:T(4,128)}, f32[3,64]{1,0:T(4,128)S(1)}, u32[]{:S(2)}) copy-start(f32[3,64]{1,0:T(4,128)S(1)} %add.267) | copy-start | bytes 2308
  134.3 76.0 %all-gather.3.cloned.1.call-start = ((), (), s32[]{:S(2)}) async-start(), calls=%async_computation.5 | async-start | bytes 1327104 | tf_op jit(solution)/shard_map/all_gather | solution.py:80
  136.0 84.2 %all-gather.5.cloned.1.call-start = ((), (), s32[]{:S(2)}) async-start(), calls=%async_computation.6 | async-start | bytes 1327104 | tf_op jit(solution)/shard_map/all_gather | solution.py:81
  137.8 166.2 %all-reduce.8.cloned.1.call-start = ((), (), s32[]{:S(2)}) async-start(), calls=%async_computation.7 | async-start | bytes 6291456 | tf_op jit(solution)/shard_map/psum | solution.py:130
  220.3 12.5 %copy-start.56 = (bf16[768,768]{1,0:T(8,128)(2,1)S(1)}, bf16[768,768]{1,0:T(8,128)(2,1)}, u32[]{:S(2)}) copy-start(bf16[768,768]{1,0:T(8,128)(2,1)} %all-gather.3.cloned.1.call-done) | copy-start | bytes 3538948
  236.9 190.5 %reduce-scatter.15.cloned.1.call-start = ((), (), s32[]{:S(2)}) async-start(), calls=%async_computation.11 | async-start | bytes 884736
  303.9 7.1 copy-start.2
  303.9 7.1 copy-start.6
  303.9 7.1 copy-start.8
  303.9 7.1 copy-start.28
  311.0 7.4 %copy-start.7 = (bf16[2048,192]{0,1:T(8,128)(2,1)S(1)}, bf16[2048,192]{0,1:T(8,128)(2,1)}, u32[]{:S(2)}) copy-start(bf16[2048,192]{0,1:T(8,128)(2,1)} %reshape.145) | copy-start | bytes 2359300
  325.6 7.0 copy-start.45
  332.6 5.1 copy-start.23
  332.6 5.1 copy-start.47
  360.5 153.4 %all-reduce.10.cloned.1.call-start = ((), (), s32[]{:S(2)}) async-start(), calls=%async_computation.12 | async-start | bytes 12582912 | tf_op jit(solution)/shard_map/psum | solution.py:121
  394.0 165.8 %reduce-scatter.9.cloned.1.call-start = ((), (), s32[]{:S(2)}) async-start(), calls=%async_computation.8 | async-start | bytes 2654208 | tf_op jit(solution)/shard_map/reduce_scatter | solution.py:176
  401.1 7.3 %copy-start.26 = (f32[2048]{0:T(1024)S(1)}, f32[2048]{0:T(1024)}, u32[]{:S(2)}) copy-start(f32[2048]{0:T(1024)} %copy-done.25) | copy-start | bytes 24580
  401.1 7.3 %copy-start.33 = (f32[2048]{0:T(1024)S(1)}, f32[2048]{0:T(1024)}, u32[]{:S(2)}) copy-start(f32[2048]{0:T(1024)} %copy-done.32) | copy-start | bytes 24580
  401.1 7.3 %copy-start.36 = (f32[768]{0:T(1024)S(1)}, f32[768]{0:T(1024)}, u32[]{:S(2)}) copy-start(f32[768]{0:T(1024)} %copy-done.35) | copy-start | bytes 9220
  401.1 7.3 %copy-start.55 = (f32[768]{0:T(1024)S(1)}, f32[768]{0:T(1024)}, u32[]{:S(2)}) copy-start(f32[768]{0:T(1024)} %copy-done.54) | copy-start | bytes 9220
  401.1 166.6 %reduce-scatter.11.cloned.1.call-start = ((), (), s32[]{:S(2)}) async-start(), calls=%async_computation.9 | async-start | bytes 2654208 | tf_op jit(solution)/shard_map/reduce_scatter | solution.py:177
  408.3 229.4 %reduce-scatter.13.cloned.1.call-start = ((), (), s32[]{:S(2)}) async-start(), calls=%async_computation.10 | async-start | bytes 2211840
  417.8 4.8 copy-start.14
  422.5 4.6 copy-start.42
  514.0 4.7 copy-start.53
  556.0 83.6 %copy-start.30 = (f32[6,768]{1,0:T(8,128)}, f32[6,768]{1,0:T(8,128)S(1)}, u32[]{:S(2)}) copy-start(f32[6,768]{1,0:T(8,128)S(1)} %get-tuple-element.136) | copy-start | bytes 55300
  556.0 83.6 %copy-start.40 = (f32[768]{0:T(1024)}, f32[768]{0:T(1024)S(1)}, u32[]{:S(2)}) copy-start(f32[768]{0:T(1024)S(1)} %get-tuple-element.138) | copy-start | bytes 9220
  556.0 83.6 %copy-start.48 = (f32[2,192]{1,0:T(2,128)}, f32[2,192]{1,0:T(2,128)S(1)}, u32[]{:S(2)}) copy-start(f32[2,192]{1,0:T(2,128)S(1)} %get-tuple-element.137) | copy-start | bytes 4612
  654.6 44.5 %copy-start.49 = (f32[2,192]{1,0:T(2,128)S(1)}, f32[2,192]{1,0:T(2,128)}, u32[]{:S(2)}) copy-start(f32[2,192]{1,0:T(2,128)} %copy-done.48) | copy-start | bytes 4612
  654.6 44.5 %copy-start.51 = (f32[2,192]{1,0:T(2,128)S(1)}, f32[2,192]{1,0:T(2,128)}, u32[]{:S(2)}) copy-start(f32[2,192]{1,0:T(2,128)} %param.42) | copy-start | bytes 4612
  654.6 45.8 %copy-start.41 = (f32[768]{0:T(1024)S(1)}, f32[768]{0:T(1024)}, u32[]{:S(2)}) copy-start(f32[768]{0:T(1024)} %copy-done.40) | copy-start | bytes 9220
  654.6 45.8 %copy-start.52 = (f32[768]{0:T(1024)S(1)}, f32[768]{0:T(1024)}, u32[]{:S(2)}) copy-start(f32[768]{0:T(1024)} %param.45) | copy-start | bytes 9220
  654.7 48.5 %copy-start.18 = (f32[192,96]{1,0:T(8,128)S(1)}, f32[192,96]{1,0:T(8,128)}, u32[]{:S(2)}) copy-start(f32[192,96]{1,0:T(8,128)} %param.30) | copy-start | bytes 221188
  654.7 48.5 %copy-start.29 = (f32[192,96]{1,0:T(8,128)S(1)}, f32[192,96]{1,0:T(8,128)}, u32[]{:S(2)}) copy-start(f32[192,96]{1,0:T(8,128)} %param.32) | copy-start | bytes 221188
  654.7 50.1 %copy-start.9 = (f32[96,768]{1,0:T(8,128)S(1)}, f32[96,768]{1,0:T(8,128)}, u32[]{:S(2)}) copy-start(f32[96,768]{1,0:T(8,128)} %param.33) | copy-start | bytes 884740
  654.7 50.1 %copy-start.11 = (f32[96,768]{1,0:T(8,128)S(1)}, f32[96,768]{1,0:T(8,128)}, u32[]{:S(2)}) copy-start(f32[96,768]{1,0:T(8,128)} %reduce-scatter.9.cloned.1.call-done) | copy-start | bytes 884740
  654.7 50.1 %copy-start.19 = (f32[96,768]{1,0:T(8,128)S(1)}, f32[96,768]{1,0:T(8,128)}, u32[]{:S(2)}) copy-start(f32[96,768]{1,0:T(8,128)} %param.35) | copy-start | bytes 884740
  654.7 50.1 %copy-start.20 = (f32[96,768]{1,0:T(8,128)S(1)}, f32[96,768]{1,0:T(8,128)}, u32[]{:S(2)}) copy-start(f32[96,768]{1,0:T(8,128)} %param.34) | copy-start | bytes 884740
  695.0 10.9 %copy-start.10 = (f32[768,96]{0,1:T(8,128)S(1)}, f32[768,96]{0,1:T(8,128)}, u32[]{:S(2)}) copy-start(f32[768,96]{0,1:T(8,128)} %param.36) | copy-start | bytes 884740
  695.0 10.9 %copy-start.12 = (f32[768,96]{0,1:T(8,128)S(1)}, f32[768,96]{0,1:T(8,128)}, u32[]{:S(2)}) copy-start(f32[768,96]{0,1:T(8,128)} %reduce-scatter.11.cloned.1.call-done) | copy-start | bytes 884740
  695.0 10.9 %copy-start.21 = (f32[768,96]{0,1:T(8,128)S(1)}, f32[768,96]{0,1:T(8,128)}, u32[]{:S(2)}) copy-start(f32[768,96]{0,1:T(8,128)} %param.38) | copy-start | bytes 884740
  696.5 9.4 %copy-start.22 = (f32[768,96]{0,1:T(8,128)S(1)}, f32[768,96]{0,1:T(8,128)}, u32[]{:S(2)}) copy-start(f32[768,96]{0,1:T(8,128)} %param.37) | copy-start | bytes 884740
  (19 other events, 59.2 us)
Sparse Core Ops, SparseCore 0:
  134.4 67.2 all-reduce.5
  237.0 66.9 all-reduce.7
  394.1 119.8 all-reduce.9
Sparse Core Ops, SparseCore 1:
  137.6 40.2 all-gather.2
  180.5 39.8 all-gather.4
  360.6 62.6 reduce-scatter.14
  427.2 68.3 reduce-scatter.8
  499.5 68.2 reduce-scatter.10
  571.6 66.1 reduce-scatter.12
where the time goes:
time: 722 us; the launch traced here: 715 us
  waiting for transfers between devices  284 us (39%)
  blocking collectives  149 us (21%)
  matrix products  103 us (14%)
  local copies, waits for them, and re-layouts  94 us (13%)
  other arithmetic  62.2 us (9%)
  between operations  22.6 us (3%)
    psum x1, waiting for transfers between devices, per_device(): fed = lax.psum(fed_part.astype(jnp.bfloat16), 'mp').astype(jnp.float32)  85 us
    unnamed x11, waiting for transfers between devices  67.4 us
    psum x1, waiting for transfers between devices, per_device(): lax.psum(attn_part.astype(jnp.bfloat16), 'mp').astype(jnp.float32)  63.8 us
    psum x1, waiting for transfers between devices, per_device(): lax.psum(second_part.astype(jnp.bfloat16), 'mp').astype(jnp.float32)  58.7 us
    all_gather x1, blocking collectives, per_device(): lax.all_gather(triple_weight.astype(bf16), 'dp', axis=1, tiled=True)  40.5 us
    psum x1, blocking collectives, per_device(): total_square = lax.psum(local_square, ('dp', 'mp'))  39.5 us
    psum x1, blocking collectives, per_device(): vectors = lax.psum((grad_norms, grad_paired, grad_hidden), 'dp')  37.3 us
    unnamed x130, local copies, waits for them, and re-layouts  32.6 us
  transfers between devices with their start and end apart: 9, of which 6 were waited for; matrix products, arithmetic and copies ran while one was open for 15% of the time, Pallas kernels for 0%

commit v1 on v0

--- a/solution.py
+++ b/solution.py
@@ -185,7 +185,9 @@
         local_square
         + (jnp.sum(vectors[1] * vectors[1]) + jnp.sum(vectors[2] * vectors[2])) / dp_count
     )
-    total_square = lax.psum(local_square, ("dp", "mp"))
+    total_square = local_square
+    for over in ("mp", "dp"):
+        total_square = lax.psum(total_square, over)
     gradient_norm = jnp.sqrt(total_square)
     factor = jnp.minimum(1.0, CLIP / gradient_norm)
     triple_new = adam_step(

time: 722 us -> 709 us (0.982)
  blocking collectives: 149 us -> 136 us
    psum x1 -> x2, blocking collectives: 39.5 us -> 25.8 us  [per_device(): total_square = lax.psum(total_square, over)]
where the time goes in v1:
time: 709 us; the launch traced here: 703 us
  waiting for transfers between devices  283 us (40%)
  blocking collectives  136 us (19%)
  matrix products  103 us (15%)
  local copies, waits for them, and re-layouts  94 us (13%)
  other arithmetic  63.4 us (9%)
  between operations  22.5 us (3%)
    psum x1, waiting for transfers between devices, per_device(): fed = lax.psum(fed_part.astype(jnp.bfloat16), 'mp').astype(jnp.float32)  85 us
    unnamed x11, waiting for transfers between devices  68 us
    psum x1, waiting for transfers between devices, per_device(): lax.psum(attn_part.astype(jnp.bfloat16), 'mp').astype(jnp.float32)  63.8 us
    psum x1, waiting for transfers between devices, per_device(): lax.psum(second_part.astype(jnp.bfloat16), 'mp').astype(jnp.float32)  58.7 us
    all_gather x1, blocking collectives, per_device(): lax.all_gather(triple_weight.astype(bf16), 'dp', axis=1, tiled=True)  40.5 us
    psum x1, blocking collectives, per_device(): vectors = lax.psum((grad_norms, grad_paired, grad_hidden), 'dp')  37.8 us
    unnamed x130, local copies, waits for them, and re-layouts  32.6 us
    all_gather x1, blocking collectives, per_device(): lax.all_gather(outward_weight.astype(bf16), 'dp', axis=1, tiled=True)  31.9 us
  transfers between devices with their start and end apart: 9, of which 6 were waited for; matrix products, arithmetic and copies ran while one was open for 15% of the time, Pallas kernels for 0%

profile of v1, /device:TPU:0, one launch (start us, length us, event | category | flops | bytes accessed | tf_op | source)
XLA Modules:
  0.0 702.9 jit_solution(3905411026837981229)
XLA Ops:
  12.8 40.5 %all_gather.12 = bf16[3,768,192]{2,0,1:T(4,128)(2,1)} all-gather(bf16[3,96,192]{2,0,1:T(4,128)(2,1)S(1)} %copy.118), channel_id=1, replica_groups=mesh['dp'=8,'mp'=4] {'dp'}, dimensions={1}, use_global_device_ids=true | all-gather | bytes 995328 | tf_op jit(solution)/shard_map/all_gather | solution.py:78
  53.2 3.4 copy.119
  56.7 3.4 fusion.96
  65.1 31.9 %all_gather.13 = bf16[192,768]{0,1:T(8,128)(2,1)S(1)} all-gather(bf16[192,96]{0,1:T(8,128)(2,1)} %copy.127), channel_id=1, replica_groups=mesh['dp'=8,'mp'=4] {'dp'}, dimensions={1}, use_global_device_ids=true | all-gather | bytes 331776 | tf_op jit(solution)/shard_map/all_gather | solution.py:79
  97.0 3.4 convert_element_type.130
  100.4 3.4 copy.123
  103.8 3.6 squeeze.4
  107.4 3.9 copy.120
  111.3 3.6 squeeze.10
  114.9 5.7 fusion.108
  126.9 3.5 reshape.145
  130.4 3.9 convolution_convert_fusion.2
  138.0 63.8 %all-reduce.6.cloned.1.call-done = bf16[2048,768]{1,0:T(8,128)(2,1)} async-done(((bf16[2048,768]{1,0:T(8,128)(2,1)}), bf16[2048,768]{1,0:T(8,128)(2,1)}) %all-reduce.6.cloned.1.call-update) | async-done | bytes 3145744 | tf_op jit(solution)/shard_map/psum | solution.py:113
  201.8 3.1 fusion.46
  210.4 7.5 %fusion.111 = f32[2048,768]{1,0:T(8,128)} fusion(bf16[2048,768]{1,0:T(8,128)(2,1)} %add_convert_fusion.1, bf16[768,768]{1,0:T(8,128)(2,1)} %all-gather.3.cloned.1.call-done), kind=kOutput, calls=%fused_computation.161 | convolution fusion | flops 2415919104 | bytes 10616832 | tf_op jit(solution)/shard_map/dot_general | solution.py:117
  220.3 10.8 %convert_reduce_fusion.4 = (f32[768]{0:T(1024)}, bf16[2048,768]{1,0:T(8,128)(2,1)S(1)}, bf16[2048,768]{1,0:T(8,128)(2,1)}) fusion(f32[2048,768]{1,0:T(8,128)} %fusion.111, f32[768]{0:T(1024)} %param.45, bf16[2048,768]{1,0:T(8,128)(2,1)} %param.26, bf16[768,768]{0,1:T(8,128)(2,1)} %all-gather.5.cloned.1.call-done), kind=kOutput, calls=%fused_computation.46 | convolution fusion | flops 2455239936 | bytes 16914432 | tf_op jit(solution)/shard_map/td,fd->tf/dot_general | solution.py:125
  232.8 4.0 convolution_convert_fusion
  238.7 6.6 convolution_convert_fusion.1
  245.2 58.7 %all-reduce.8.cloned.1.call-done = bf16[2048,768]{1,0:T(8,128)(2,1)} async-done(((bf16[2048,768]{1,0:T(8,128)(2,1)}), bf16[2048,768]{1,0:T(8,128)(2,1)}) %all-reduce.8.cloned.1.call-update) | async-done | bytes 3145744 | tf_op jit(solution)/shard_map/psum | solution.py:130
  303.9 7.1 %fusion.30 = (f32[768]{0:T(1024)}, f32[2048]{0:T(1024)S(1)}, f32[2048]{0:T(1024)S(1)}, f32[768]{0:T(1024)}) fusion(bf16[2048,768]{1,0:T(8,128)(2,1)} %all-reduce.8.cloned.1.call-done, f32[2048]{0:T(1024)} %copy-done.27, f32[2048]{0:T(1024)S(1)} %broadcast_multiply_fusion.4, f32[768]{0:T(1024)S(1)} %get-tuple-element.131, ...), kind=kLoop, calls=%fused_computation.43 | loop fusion | flops 22014464 | bytes 9482240 | tf_op jit(solution)/shard_map/reduce_sum | solution.py:167
  311.1 4.7 fusion.106
  320.7 4.9 convolution_convert_fusion.3
  325.6 3.4 reshape.146
  329.0 3.6 copy.128
  332.7 5.1 fusion.81
  337.8 10.3 %fusion.71 = bf16[32,64,3,64]{1,3,2,0:T(8,128)(2,1)} fusion(f32[32,3,64,64]{2,3,1,0:T(8,128)} %fusion.81, f32[32,3,64,64]{2,3,1,0:T(8,128)} %copy-done.4, f32[32,3,64]{2,1,0:T(4,128)S(1)} %copy-done.23, f32[32,64,3,64]{1,0,3,2:T(8,128)} %squeeze.10, f32[3,64]{1,0:T(4,128)S(1)} %copy-done.47), kind=kOutput, calls=%fused_computation.91 | convolution fusion | flops 54270016 | bytes 5530368 | tf_op jit(solution)/shard_map/rhqk,rqhd->rkhd/dot_general | solution.py:150
  348.1 8.1 %convert_reduce_fusion.6 = (f32[3,64]{1,0:T(4,128)S(1)}, bf16[32,64,3,64]{3,1,2,0:T(8,128)(2,1)}) fusion(bf16[32,64,3,64]{3,1,2,0:T(8,128)(2,1)} %copy.123, f32[32,3,64,64]{2,3,1,0:T(8,128)} %fusion.81, f32[32,3,64,64]{2,3,1,0:T(8,128)} %copy-done.4, f32[32,3,64]{2,1,0:T(4,128)S(1)} %copy-done.23), kind=kOutput, calls=%fused_computation.60 | convolution fusion | flops 54269824 | bytes 4743936 | tf_op jit(solution)/shard_map/rhqk,rkhd->rqhd/dot_general | solution.py:147
  356.2 4.4 convert_reduce_fusion.5
  360.6 3.6 copy.131
  364.2 3.5 stack.42
  369.9 3.6 copy.133
  373.4 3.5 stack.43
  377.0 3.2 copy.135
  380.1 3.5 stack.44
  387.9 6.0 bitcast_convert_fusion
  394.0 7.1 %fusion.112 = f32[768,768]{1,0:T(8,128)} fusion(bf16[2048,768]{1,0:T(8,128)(2,1)} %add_convert_fusion.1, bf16[2048,768]{1,0:T(8,128)(2,1)} %copy-done.57), kind=kOutput, calls=%fused_computation.162 | convolution fusion | flops 2415919104 | bytes 8650752 | tf_op jit(solution)/shard_map/td,tf->df/dot_general | solution.py:127
  401.4 6.9 fusion.113
  408.4 5.2 fusion.65
  413.6 4.2 copy.149
  417.8 4.7 reshape.151
  429.0 85.0 %all-reduce.10.cloned.1.call-done = (bf16[2048,768]{1,0:T(8,128)(2,1)}, bf16[2048,768]{1,0:T(8,128)(2,1)}) async-done(((bf16[2048,768]{1,0:T(8,128)(2,1)}, bf16[2048,768]{1,0:T(8,128)(2,1)}), (bf16[2048,768]{1,0:T(8,128)(2,1)}, bf16[2048,768]{1,0:T(8,128)(2,1)})) %all-reduce.10.cloned.1.call-update) | async-done | bytes 6291472 | tf_op jit(solution)/shard_map/psum | solution.py:121
  514.0 5.2 fusion.31
  519.3 37.8 %all-reduce = (f32[6,768]{1,0:T(8,128)S(1)}, f32[2,192]{1,0:T(2,128)S(1)}, f32[768]{0:T(1024)S(1)}) all-reduce(f32[6,768]{1,0:T(8,128)S(1)} %stack.52, f32[2,192]{1,0:T(2,128)S(1)} %pad_maximum_fusion, f32[768]{0:T(1024)S(1)} %copy-done.53), channel_id=1, replica_groups=mesh['dp'=8,'mp'=4] {'dp'}, use_global_device_ids=true, to_apply=%region_29.30 | all-reduce | flops 5760 | bytes 46080 | tf_op jit(solution)/shard_map/psum | solution.py:179
  562.6 5.0 reduce-scatter.11.cloned.1.call-done
  569.8 67.9 %reduce-scatter.13.cloned.1.call-done = f32[96,576]{1,0:T(8,128)} async-done(((f32[768,576]{1,0:T(8,128)}), f32[96,576]{1,0:T(8,128)}) %reduce-scatter.13.cloned.1.call-update) | async-done | bytes 221200
  645.3 6.1 psum.70
  651.4 10.5 %fusion.16 = (bf16[2048,768]{1,0:T(8,128)(2,1)}, bf16[2048,768]{1,0:T(8,128)(2,1)}) fusion(f32[2048,768]{1,0:T(8,128)} %copy-done.3, bf16[2048,768]{1,0:T(8,128)(2,1)S(1)} %copy-done, bf16[2048,768]{1,0:T(8,128)(2,1)} %get-tuple-element.140, f32[2048]{0:T(1024)} %broadcast_multiply_fusion, f32[2048]{0:T(1024)} %broadcast_multiply_fusion.1, ...), kind=kLoop, calls=%fused_computation.29 | loop fusion | flops 28311552 | bytes 25207808 | tf_op jit(solution)/shard_map/convert_element_type | solution.py:162
  662.1 19.7 %psum.71 = f32[]{:T(128)} all-reduce(f32[]{:T(128)} %psum.70), channel_id=1, replica_groups=mesh['dp'=8,'mp'=4] {'dp'}, use_global_device_ids=true, to_apply=%region_39.40 | all-reduce | flops 1 | bytes 8 | tf_op jit(solution)/shard_map/psum | solution.py:190
  (202 shorter events, 71.8 us)
Async XLA Ops:
  8.1 193.7 %all-reduce.6.cloned.1.call-start = ((), (), s32[]{:S(2)}) async-start(), calls=%async_computation.4 | async-start | bytes 6291456 | tf_op jit(solution)/shard_map/psum | solution.py:113
  10.9 45.8 %copy-start.25 = (f32[2048]{0:T(1024)}, f32[2048]{0:T(1024)S(1)}, u32[]{:S(2)}) copy-start(f32[2048]{0:T(1024)S(1)} %broadcast_multiply_fusion.5) | copy-start | bytes 24580
  12.0 48.1 %copy-start.32 = (f32[2048]{0:T(1024)}, f32[2048]{0:T(1024)S(1)}, u32[]{:S(2)}) copy-start(f32[2048]{0:T(1024)S(1)} %add_rsqrt_fusion.1) | copy-start | bytes 24580
  12.6 47.5 %copy-start.35 = (f32[768]{0:T(1024)}, f32[768]{0:T(1024)S(1)}, u32[]{:S(2)}) copy-start(f32[768]{0:T(1024)S(1)} %get-tuple-element.133) | copy-start | bytes 9220
  12.6 47.5 %copy-start.54 = (f32[768]{0:T(1024)}, f32[768]{0:T(1024)S(1)}, u32[]{:S(2)}) copy-start(f32[768]{0:T(1024)S(1)} %get-tuple-element.132) | copy-start | bytes 9220
  63.2 58.3 %copy-start.44 = (f32[3,64]{1,0:T(4,128)}, f32[3,64]{1,0:T(4,128)S(1)}, u32[]{:S(2)}) copy-start(f32[3,64]{1,0:T(4,128)S(1)} %add.266) | copy-start | bytes 2308
  63.3 51.6 %copy-start.46 = (f32[3,64]{1,0:T(4,128)}, f32[3,64]{1,0:T(4,128)S(1)}, u32[]{:S(2)}) copy-start(f32[3,64]{1,0:T(4,128)S(1)} %add.269) | copy-start | bytes 2308
  134.3 76.0 %all-gather.3.cloned.1.call-start = ((), (), s32[]{:S(2)}) async-start(), calls=%async_computation.5 | async-start | bytes 1327104 | tf_op jit(solution)/shard_map/all_gather | solution.py:80
  136.0 84.2 %all-gather.5.cloned.1.call-start = ((), (), s32[]{:S(2)}) async-start(), calls=%async_computation.6 | async-start | bytes 1327104 | tf_op jit(solution)/shard_map/all_gather | solution.py:81
  137.8 166.2 %all-reduce.8.cloned.1.call-start = ((), (), s32[]{:S(2)}) async-start(), calls=%async_computation.7 | async-start | bytes 6291456 | tf_op jit(solution)/shard_map/psum | solution.py:130
  220.3 12.5 %copy-start.56 = (bf16[768,768]{1,0:T(8,128)(2,1)S(1)}, bf16[768,768]{1,0:T(8,128)(2,1)}, u32[]{:S(2)}) copy-start(bf16[768,768]{1,0:T(8,128)(2,1)} %all-gather.3.cloned.1.call-done) | copy-start | bytes 3538948
  236.9 190.5 %reduce-scatter.15.cloned.1.call-start = ((), (), s32[]{:S(2)}) async-start(), calls=%async_computation.11 | async-start | bytes 884736
  303.9 7.1 %copy-start.2 = (bf16[2048,768]{1,0:T(8,128)(2,1)S(1)}, bf16[2048,768]{1,0:T(8,128)(2,1)}, u32[]{:S(2)}) copy-start(bf16[2048,768]{1,0:T(8,128)(2,1)} %all-reduce.6.cloned.1.call-done) | copy-start | bytes 9437188
  303.9 7.1 %copy-start.6 = (bf16[2048,768]{1,0:T(8,128)(2,1)S(1)}, bf16[2048,768]{1,0:T(8,128)(2,1)}, u32[]{:S(2)}) copy-start(bf16[2048,768]{1,0:T(8,128)(2,1)} %all-reduce.8.cloned.1.call-done) | copy-start | bytes 9437188
  303.9 7.1 %copy-start.8 = (bf16[2048,768]{1,0:T(8,128)(2,1)S(1)}, bf16[2048,768]{1,0:T(8,128)(2,1)}, u32[]{:S(2)}) copy-start(bf16[2048,768]{1,0:T(8,128)(2,1)} %param.26) | copy-start | bytes 9437188
  303.9 7.1 %copy-start.28 = (f32[2048]{0:T(1024)S(1)}, f32[2048]{0:T(1024)}, u32[]{:S(2)}) copy-start(f32[2048]{0:T(1024)} %copy-done.27) | copy-start | bytes 24580
  311.0 7.4 %copy-start.7 = (bf16[2048,192]{0,1:T(8,128)(2,1)S(1)}, bf16[2048,192]{0,1:T(8,128)(2,1)}, u32[]{:S(2)}) copy-start(bf16[2048,192]{0,1:T(8,128)(2,1)} %reshape.145) | copy-start | bytes 2359300
  325.6 7.0 copy-start.45
  332.6 5.1 copy-start.23
  332.6 5.1 copy-start.47
  360.5 153.4 %all-reduce.10.cloned.1.call-start = ((), (), s32[]{:S(2)}) async-start(), calls=%async_computation.12 | async-start | bytes 12582912 | tf_op jit(solution)/shard_map/psum | solution.py:121
  394.0 167.0 %reduce-scatter.9.cloned.1.call-start = ((), (), s32[]{:S(2)}) async-start(), calls=%async_computation.8 | async-start | bytes 2654208 | tf_op jit(solution)/shard_map/reduce_scatter | solution.py:176
  401.1 7.3 %copy-start.26 = (f32[2048]{0:T(1024)S(1)}, f32[2048]{0:T(1024)}, u32[]{:S(2)}) copy-start(f32[2048]{0:T(1024)} %copy-done.25) | copy-start | bytes 24580
  401.1 7.3 %copy-start.33 = (f32[2048]{0:T(1024)S(1)}, f32[2048]{0:T(1024)}, u32[]{:S(2)}) copy-start(f32[2048]{0:T(1024)} %copy-done.32) | copy-start | bytes 24580
  401.1 7.3 %copy-start.36 = (f32[768]{0:T(1024)S(1)}, f32[768]{0:T(1024)}, u32[]{:S(2)}) copy-start(f32[768]{0:T(1024)} %copy-done.35) | copy-start | bytes 9220
  401.1 7.3 %copy-start.55 = (f32[768]{0:T(1024)S(1)}, f32[768]{0:T(1024)}, u32[]{:S(2)}) copy-start(f32[768]{0:T(1024)} %copy-done.54) | copy-start | bytes 9220
  401.1 166.4 %reduce-scatter.11.cloned.1.call-start = ((), (), s32[]{:S(2)}) async-start(), calls=%async_computation.9 | async-start | bytes 2654208 | tf_op jit(solution)/shard_map/reduce_scatter | solution.py:177
  408.3 229.3 %reduce-scatter.13.cloned.1.call-start = ((), (), s32[]{:S(2)}) async-start(), calls=%async_computation.10 | async-start | bytes 2211840
  417.8 4.8 copy-start.14
  422.5 4.6 copy-start.42
  514.0 5.3 copy-start.53
  557.1 82.4 %copy-start.30 = (f32[6,768]{1,0:T(8,128)}, f32[6,768]{1,0:T(8,128)S(1)}, u32[]{:S(2)}) copy-start(f32[6,768]{1,0:T(8,128)S(1)} %get-tuple-element.136) | copy-start | bytes 55300
  557.1 82.4 %copy-start.40 = (f32[768]{0:T(1024)}, f32[768]{0:T(1024)S(1)}, u32[]{:S(2)}) copy-start(f32[768]{0:T(1024)S(1)} %get-tuple-element.138) | copy-start | bytes 9220
  557.1 82.4 %copy-start.48 = (f32[2,192]{1,0:T(2,128)}, f32[2,192]{1,0:T(2,128)S(1)}, u32[]{:S(2)}) copy-start(f32[2,192]{1,0:T(2,128)S(1)} %get-tuple-element.137) | copy-start | bytes 4612
  661.9 24.6 %copy-start.49 = (f32[2,192]{1,0:T(2,128)S(1)}, f32[2,192]{1,0:T(2,128)}, u32[]{:S(2)}) copy-start(f32[2,192]{1,0:T(2,128)} %copy-done.48) | copy-start | bytes 4612
  661.9 24.6 %copy-start.51 = (f32[2,192]{1,0:T(2,128)S(1)}, f32[2,192]{1,0:T(2,128)}, u32[]{:S(2)}) copy-start(f32[2,192]{1,0:T(2,128)} %param.42) | copy-start | bytes 4612
  662.0 25.9 %copy-start.41 = (f32[768]{0:T(1024)S(1)}, f32[768]{0:T(1024)}, u32[]{:S(2)}) copy-start(f32[768]{0:T(1024)} %copy-done.40) | copy-start | bytes 9220
  662.0 25.9 %copy-start.52 = (f32[768]{0:T(1024)S(1)}, f32[768]{0:T(1024)}, u32[]{:S(2)}) copy-start(f32[768]{0:T(1024)} %param.45) | copy-start | bytes 9220
  662.0 28.7 %copy-start.18 = (f32[192,96]{1,0:T(8,128)S(1)}, f32[192,96]{1,0:T(8,128)}, u32[]{:S(2)}) copy-start(f32[192,96]{1,0:T(8,128)} %param.30) | copy-start | bytes 221188
  662.0 28.6 %copy-start.29 = (f32[192,96]{1,0:T(8,128)S(1)}, f32[192,96]{1,0:T(8,128)}, u32[]{:S(2)}) copy-start(f32[192,96]{1,0:T(8,128)} %param.32) | copy-start | bytes 221188
  662.0 30.3 %copy-start.9 = (f32[96,768]{1,0:T(8,128)S(1)}, f32[96,768]{1,0:T(8,128)}, u32[]{:S(2)}) copy-start(f32[96,768]{1,0:T(8,128)} %param.33) | copy-start | bytes 884740
  662.0 30.3 %copy-start.11 = (f32[96,768]{1,0:T(8,128)S(1)}, f32[96,768]{1,0:T(8,128)}, u32[]{:S(2)}) copy-start(f32[96,768]{1,0:T(8,128)} %reduce-scatter.9.cloned.1.call-done) | copy-start | bytes 884740
  662.0 30.3 %copy-start.19 = (f32[96,768]{1,0:T(8,128)S(1)}, f32[96,768]{1,0:T(8,128)}, u32[]{:S(2)}) copy-start(f32[96,768]{1,0:T(8,128)} %param.35) | copy-start | bytes 884740
  662.0 30.3 %copy-start.20 = (f32[96,768]{1,0:T(8,128)S(1)}, f32[96,768]{1,0:T(8,128)}, u32[]{:S(2)}) copy-start(f32[96,768]{1,0:T(8,128)} %param.34) | copy-start | bytes 884740
  682.5 10.9 %copy-start.10 = (f32[768,96]{0,1:T(8,128)S(1)}, f32[768,96]{0,1:T(8,128)}, u32[]{:S(2)}) copy-start(f32[768,96]{0,1:T(8,128)} %param.36) | copy-start | bytes 884740
  682.5 10.9 %copy-start.12 = (f32[768,96]{0,1:T(8,128)S(1)}, f32[768,96]{0,1:T(8,128)}, u32[]{:S(2)}) copy-start(f32[768,96]{0,1:T(8,128)} %reduce-scatter.11.cloned.1.call-done) | copy-start | bytes 884740
  682.5 10.9 %copy-start.21 = (f32[768,96]{0,1:T(8,128)S(1)}, f32[768,96]{0,1:T(8,128)}, u32[]{:S(2)}) copy-start(f32[768,96]{0,1:T(8,128)} %param.38) | copy-start | bytes 884740
  683.9 9.4 %copy-start.22 = (f32[768,96]{0,1:T(8,128)S(1)}, f32[768,96]{0,1:T(8,128)}, u32[]{:S(2)}) copy-start(f32[768,96]{0,1:T(8,128)} %param.37) | copy-start | bytes 884740
  (19 other events, 59.2 us)
Sparse Core Ops, SparseCore 0:
  134.4 67.2 all-reduce.5
  237.0 66.9 all-reduce.7
  394.1 119.8 all-reduce.9
Sparse Core Ops, SparseCore 1:
  137.6 40.2 all-gather.2
  180.5 39.8 all-gather.4
  360.6 62.6 reduce-scatter.14
  427.2 68.3 reduce-scatter.8
  499.5 68.0 reduce-scatter.10
  571.5 66.1 reduce-scatter.12
